TPU v7x, 256 devices: a whole 4x4x8 slice. The times are simulated.
256 devices in a mesh: ctx: 64 (over y, z_lo, x, core), tp: 4 (over z_hi).
Axes of the slice: x: 4, y: 4, z: 8 (z_hi: 4, z_lo: 2; z = z_hi * 2 + z_lo), core: 2. Of those that a mesh axis runs over, the one named last changes fastest.
Arguments:
- queries: bfloat16 [16384, 2048], P('ctx', 'tp'), may hold values from -8 to 8
- span_keys: bfloat16 [16384, 1024], P('ctx', 'tp'), may hold values from -6 to 6
- span_values: bfloat16 [16384, 1024], P('ctx', 'tp'), may hold values from -6 to 6
- cache_keys: bfloat16 [8192, 1024], P('ctx', 'tp'), may hold values from -8 to 8
- cache_values: bfloat16 [8192, 1024], P('ctx', 'tp'), may hold values from -6 to 6
- out_weight: bfloat16 [2048, 3840], P('tp'), may hold values from -0.125 to 0.125
- offsets: int32 [64], replicated, may hold values from 0 to 16128, as said below
- earlier_block_slot: int32 [128], replicated, may hold values from 0 to 127, each once
- prior_block_count: int32 [1], replicated, may hold values from 32 to 127
Outputs:
- projected: bfloat16 [16384, 3840], P('ctx', 'tp')
Inputs may be any that keep to these rules, and one draw needn't show every extreme that they name: `offsets`: a permutation of the multiples of 256 below 16384. Block b of the earlier prompt lies in slot earlier_block_slot[b]; slot s is held by index s // 2 of ctx; only blocks below prior_block_count[0] are valid.
All inputs are finite; a program needn't handle non-finite values.
Results may differ from a plain program's by a relative error of at most 0.012.
Values may be sent and summed in bfloat16 or wider, within the bound.
No kernel may reach another device: no remote copies, remote signals or barrier semaphores. Data moves between devices by JAX's collectives and lax.ppermute only.
A program may use at most 192 MiB of HBM per device.

v0:
```python
import jax
import jax.numpy as jnp
from jax import lax
from jax.sharding import PartitionSpec as P

E = 256
BLK = 64


def per_device(
    queries,
    span_keys,
    span_values,
    cache_keys,
    cache_values,
    out_weight,
    offsets,
    earlier_block_slot,
    prior_block_count,
):
    local_tokens = queries.shape[0]
    kv_local = span_keys.shape[1] // E
    q_local = queries.shape[1] // E
    query_group_width = q_local // kv_local
    query_rows = query_group_width * local_tokens
    shard_count = lax.axis_size("ctx")
    my_shard = lax.axis_index("ctx")
    shard_ids = jnp.arange(shard_count, dtype=jnp.int32)
    my_offset = jnp.sum(jnp.where(shard_ids == my_shard, offsets, 0))
    query_pos = my_offset + jnp.arange(local_tokens, dtype=jnp.int32)
    row_pos = jnp.tile(query_pos, query_group_width)
    slot_count = earlier_block_slot.shape[0]
    slot_ids = jnp.arange(slot_count, dtype=jnp.int32)
    slot_owner_block = jnp.sum(
        jnp.where(earlier_block_slot[None, :] == slot_ids[:, None], slot_ids[None, :], 0), axis=1
    )
    live_slot = slot_owner_block < prior_block_count[0]
    grouped = (
        queries.reshape(local_tokens, kv_local, query_group_width, E)
        .transpose(1, 2, 0, 3)
        .reshape(kv_local, query_rows, E)
    )
    scale = E ** (-0.5)

    def absorb(carry, key_rows, value_rows, allowed):
        largest, total, summed = carry
        new_largest, new_total, new_summed = ([], [], [])
        scores = (
            jnp.einsum("re,ne->rn", grouped[0], key_rows, preferred_element_type=jnp.float32)
            * scale
        )
        scores = jnp.where(allowed, scores, -1e30)
        peak = jnp.maximum(largest[0], jnp.max(scores, axis=1))
        weights = jnp.where(allowed, jnp.exp(scores - peak[:, None]), 0.0)
        factor = jnp.exp(largest[0] - peak)
        new_largest.append(peak)
        new_total.append(total[0] * factor + jnp.sum(weights, axis=1))
        update = jnp.dot(
            weights.astype(jnp.bfloat16), value_rows, preferred_element_type=jnp.float32
        )
        new_summed.append(summed[0] * factor[:, None] + update)
        return (jnp.stack(new_largest), jnp.stack(new_total), jnp.stack(new_summed))

    def guarded(carry, key_rows, value_rows, allowed):
        return absorb(carry, key_rows, value_rows, allowed)

    initial = (
        jnp.full((kv_local, query_rows), -1e30, jnp.float32),
        jnp.zeros((kv_local, query_rows), jnp.float32),
        jnp.zeros((kv_local, query_rows, E), jnp.float32),
    )
    key_rows = lax.all_gather(cache_keys, "ctx", axis=0, tiled=True)
    value_rows = lax.all_gather(cache_values, "ctx", axis=0, tiled=True)
    row_count = key_rows.shape[0]
    slot_number = jnp.arange(row_count, dtype=jnp.int32) // BLK
    allowed = jnp.broadcast_to(
        jnp.any((slot_number[:, None] == slot_ids[None, :]) & live_slot[None, :], axis=1)[None, :],
        (query_rows, row_count),
    )
    state = guarded(initial, key_rows, value_rows, allowed)
    key_rows = lax.all_gather(span_keys, "ctx", axis=0, tiled=True)
    value_rows = lax.all_gather(span_values, "ctx", axis=0, tiled=True)
    row_count = key_rows.shape[0]
    global_row = jnp.arange(row_count, dtype=jnp.int32)
    key_pos = (
        jnp.sum(
            jnp.where(
                (global_row // local_tokens)[:, None] == shard_ids[None, :], offsets[None, :], 0
            ),
            axis=1,
        )
        + global_row % local_tokens
    )
    allowed = key_pos[None, :] <= row_pos[:, None]
    state = guarded(state, key_rows, value_rows, allowed)
    largest, total, summed = state
    attended = summed / total[:, :, None]
    attended = (
        attended.reshape(kv_local, query_group_width, local_tokens, E)
        .transpose(2, 0, 1, 3)
        .reshape(local_tokens, q_local * E)
        .astype(jnp.bfloat16)
    )
    partial_out = jnp.dot(attended, out_weight, preferred_element_type=jnp.float32)
    return lax.psum_scatter(partial_out.astype(jnp.bfloat16), "tp", scatter_dimension=1, tiled=True)


def solution(mesh):
    placed = (
        P("ctx", "tp"),
        P("ctx", "tp"),
        P("ctx", "tp"),
        P("ctx", "tp"),
        P("ctx", "tp"),
        P("tp", None),
        P(),
        P(),
        P(),
    )
    return jax.shard_map(
        per_device, mesh=mesh, in_specs=placed, out_specs=P("ctx", "tp"), check_vma=False
    )
```

profile of v0, /device:TPU:1, one launch (start us, length us, event | category | flops | bytes accessed | tf_op | source)
XLA Modules:
  0.0 531.4 jit_solution(16656678070115511567)
XLA Ops:
  6.5 0.0 all-gather.5.cloned.1.call-start
  6.5 0.7 all-gather.5.cloned.1.call-update
  7.3 0.0 all-gather.9.cloned.1.call-start
  7.3 0.7 all-gather.9.cloned.1.call-update
  8.0 0.0 all-gather.7.cloned.1.call-start
  8.1 0.7 all-gather.7.cloned.1.call-update
  8.7 0.0 all-gather.11.cloned.1.call-start
  8.8 0.5 all-gather.11.cloned.1.call-update
  9.3 0.0 reduce-scatter.2.cloned.1.call-start
  9.4 1.3 fusion.39
  10.7 0.6 iota_add_fusion
  11.3 1.1 copy.14
  12.4 0.1 copy.15
  13.2 0.8 select_reduce_fusion.1
  14.0 2.6 fusion.12
  16.6 1.4 select_reduce_fusion
  18.0 103.0 %all-gather.5.cloned.1.call-done = bf16[8192,256]{1,0:T(8,128)(2,1)} async-done(((bf16[128,256]{1,0:T(8,128)(2,1)}), bf16[8192,256]{1,0:T(8,128)(2,1)}) %all-gather.5.cloned.1.call-update) | async-done | bytes 4194320 | tf_op jit(solution)/shard_map/all_gather | solution.py:72
  121.0 9.4 %fusion.5 = (f32[512]{0:T(512)S(1)}, f32[512,8192]{1,0:T(8,128)}) fusion(pred[8192]{0:T(1024)(128)(4,1)S(1)} %fusion.12, bf16[512,256]{1,0:T(8,128)(2,1)S(1)} %bitcast.23, bf16[8192,256]{1,0:T(8,128)(2,1)} %all-gather.5.cloned.1.call-done), kind=kOutput, calls=%fused_computation.8 | convolution fusion | flops 2160066048 | bytes 21243904 | tf_op jit(solution)/shard_map/re,ne->rn/dot_general | solution.py:49
  130.4 104.0 %all-gather.9.cloned.1.call-done = bf16[16384,256]{1,0:T(8,128)(2,1)} async-done(((bf16[256,256]{1,0:T(8,128)(2,1)}), bf16[16384,256]{1,0:T(8,128)(2,1)}) %all-gather.9.cloned.1.call-update) | async-done | bytes 8388624 | tf_op jit(solution)/shard_map/all_gather | solution.py:81
  234.4 17.2 %fusion = (f32[512]{0:T(512)S(1)}, f32[512,16384]{1,0:T(8,128)}) fusion(s32[16384]{0:T(1024)S(1)} %fusion.34, s32[512]{0:T(512)S(1)} %bitcast.26, bf16[512,256]{1,0:T(8,128)(2,1)S(1)} %bitcast.24, bf16[16384,256]{1,0:T(8,128)(2,1)} %all-gather.9.cloned.1.call-done), kind=kOutput, calls=%fused_computation.2 | convolution fusion | flops 4328521216 | bytes 42274816 | tf_op jit(solution)/shard_map/re,ne->rn/dot_general | solution.py:49
  251.6 8.6 %fusion.6 = f32[512]{0:T(512)S(1)} fusion(f32[512,8192]{1,0:T(8,128)} %get-tuple-element.11, f32[512]{0:T(512)S(1)} %get-tuple-element.9, pred[8192]{0:T(1024)(128)(4,1)S(1)} %fusion.12), kind=kLoop, calls=%fused_computation.9 | loop fusion | flops 20971008 | bytes 16789504 | tf_op jit(solution)/shard_map/reduce_sum | solution.py:57
  260.2 15.9 %fusion.1 = f32[512]{0:T(512)S(1)} fusion(f32[512,16384]{1,0:T(8,128)} %get-tuple-element.13, f32[512]{0:T(512)S(1)} %get-tuple-element.8, s32[16384]{0:T(1024)S(1)} %fusion.34, s32[512]{0:T(512)S(1)} %bitcast.27), kind=kLoop, calls=%fused_computation.3 | loop fusion | flops 50331136 | bytes 33626112 | tf_op jit(solution)/shard_map/reduce_sum | solution.py:57
  276.1 66.8 %all-gather.7.cloned.1.call-done = bf16[8192,256]{1,0:T(8,128)(2,1)} async-done(((bf16[128,256]{1,0:T(8,128)(2,1)}), bf16[8192,256]{1,0:T(8,128)(2,1)}) %all-gather.7.cloned.1.call-update) | async-done | bytes 4194320 | tf_op jit(solution)/shard_map/all_gather | solution.py:73
  342.9 8.8 %fusion.19 = f32[512,256]{1,0:T(8,128)S(1)} fusion(bf16[8192,256]{1,0:T(8,128)(2,1)} %all-gather.7.cloned.1.call-done, f32[512,8192]{1,0:T(8,128)} %get-tuple-element.11, f32[512]{0:T(512)S(1)} %get-tuple-element.9, pred[8192]{0:T(1024)(128)(4,1)S(1)} %fusion.12, f32[512]{0:T(512)S(1)} %get-tuple-element.6, f32[512]{0:T(512)S(1)} %get-tuple-element.7), kind=kOutput, calls=%fused_computation.21 | convolution fusion | flops 2168717312 | bytes 21510144 | tf_op jit(solution)/shard_map/dot_general | solution.py:58
  351.7 104.4 %all-gather.11.cloned.1.call-done = bf16[16384,256]{1,0:T(8,128)(2,1)} async-done(((bf16[256,256]{1,0:T(8,128)(2,1)}), bf16[16384,256]{1,0:T(8,128)(2,1)}) %all-gather.11.cloned.1.call-update) | async-done | bytes 8388624 | tf_op jit(solution)/shard_map/all_gather | solution.py:82
  456.1 16.8 %fusion.25 = bf16[512,256]{1,0:T(8,128)(2,1)S(1)} fusion(f32[512,256]{1,0:T(8,128)S(1)} %fusion.19, bf16[16384,256]{1,0:T(8,128)(2,1)} %all-gather.11.cloned.1.call-done, f32[512,16384]{1,0:T(8,128)} %get-tuple-element.13, f32[512]{0:T(512)S(1)} %get-tuple-element.8, s32[16384]{0:T(1024)S(1)} %fusion.34, s32[512]{0:T(512)S(1)} %bitcast.28, ...), kind=kOutput, calls=%fused_computation.23 | convolution fusion | flops 4345692160 | bytes 42801152 | tf_op jit(solution)/shard_map/dot_general | solution.py:58
  472.9 0.1 copy.16
  473.0 5.0 convolution_convert_fusion
  478.1 0.0 reduce-scatter.2.cloned.1.call-update
  478.1 46.8 %reduce-scatter.2.cloned.1.call-done = bf16[256,960]{0,1:T(8,128)(2,1)} async-done(((bf16[256,3840]{0,1:T(8,128)(2,1)}), bf16[256,960]{0,1:T(8,128)(2,1)}) %reduce-scatter.2.cloned.1.call-update) | async-done | bytes 491536 | tf_op jit(solution)/shard_map/reduce_scatter | solution.py:105
  (8 shorter events, 0.1 us)
Async XLA Ops:
  6.5 114.5 %all-gather.5.cloned.1.call-start = ((), (), s32[]{:S(2)}) async-start(), calls=%async_computation.1 | async-start | bytes 4259840 | tf_op jit(solution)/shard_map/all_gather | solution.py:72
  7.3 227.1 %all-gather.9.cloned.1.call-start = ((), (), s32[]{:S(2)}) async-start(), calls=%async_computation.3 | async-start | bytes 8519680 | tf_op jit(solution)/shard_map/all_gather | solution.py:81
  8.0 334.9 %all-gather.7.cloned.1.call-start = ((), (), s32[]{:S(2)}) async-start(), calls=%async_computation.2 | async-start | bytes 4259840 | tf_op jit(solution)/shard_map/all_gather | solution.py:73
  8.7 447.4 %all-gather.11.cloned.1.call-start = ((), (), s32[]{:S(2)}) async-start(), calls=%async_computation.4 | async-start | bytes 8519680 | tf_op jit(solution)/shard_map/all_gather | solution.py:82
  9.3 515.6 %reduce-scatter.2.cloned.1.call-start = ((), (), s32[]{:S(2)}) async-start(), calls=%async_computation.5 | async-start | bytes 2457600 | tf_op jit(solution)/shard_map/reduce_scatter | solution.py:105
Sparse Core Ops, SparseCore 0:
  9.2 111.7 all-gather.4
  122.9 111.4 all-gather.8
  236.3 106.5 all-gather.6
  344.6 111.4 all-gather.10
  478.2 46.6 reduce-scatter.1
where the time goes:
time: 532 us; the launch traced here: 531 us
  waiting for transfers between devices  428 us (80%)
  matrix products  57.2 us (11%)
  other arithmetic  31.2 us (6%)
  between operations  13.9 us (3%)
    all_gather x1, waiting for transfers between devices, per_device(): value_rows = lax.all_gather(span_values, 'ctx', axis=0, tiled=True)  104 us
    all_gather x1, waiting for transfers between devices, per_device(): key_rows = lax.all_gather(span_keys, 'ctx', axis=0, tiled=True)  104 us
    all_gather x1, waiting for transfers between devices, per_device(): key_rows = lax.all_gather(cache_keys, 'ctx', axis=0, tiled=True)  103 us
    all_gather x1, waiting for transfers between devices, per_device(): value_rows = lax.all_gather(cache_values, 'ctx', axis=0, tiled=True)  66.8 us
    reduce_scatter x1, waiting for transfers between devices, per_device(): lax.psum_scatter(partial_out.astype(jnp.bfloat16), 'tp', scatter_dimensio...  46.8 us
    dot_general x2, matrix products, absorb(): jnp.einsum('re,ne->rn', grouped[0], key_rows, preferred_element_type=jnp....  26.6 us
    dot_general x2, matrix products, absorb(): jnp.dot(weights.astype(jnp.bfloat16), value_rows, preferred_element_type=...  25.6 us
    reduce_sum x2, other arithmetic, absorb(): new_total.append(total[0] * factor + jnp.sum(weights, axis=1))  24.5 us
  transfers between devices with their start and end apart: 5, of which 5 were waited for; matrix products, arithmetic and copies ran while one was open for 13% of the time, Pallas kernels for 0%

commit v1 on v0

v1 whole, which is shorter than its diff:
```python
import functools

import numpy as np
import jax
import jax.numpy as jnp
from jax import lax
from jax.experimental import pallas as pl
from jax.experimental.pallas import tpu as pltpu
from jax.sharding import PartitionSpec as P


E = 256
BLK = 64
T = 256
CB = 128
DR = T + CB
NY, NZ, NX, NC = 4, 2, 4, 2
C = np.float32(1.4426950408889634 / 16.0)
LOW = -1e30
OUT = -2e30
TK = 512
UN = 4
H = T // 2
ST = 16


def _ctx(y, z, x, c):
    return (((y % NY) * NZ + z % NZ) * NX + x % NX) * NC + c % NC


def _send(a, dy=0, fz=0, fx=0, fc=0):
    pairs = [
        (_ctx(y, z, x, c), _ctx(y + dy, z ^ fz, x ^ fx, c ^ fc))
        for y in range(NY)
        for z in range(NZ)
        for x in range(NX)
        for c in range(NC)
    ]
    return lax.ppermute(a, "ctx", pairs)


def _swap(a, axis):
    if axis == "tp":
        return lax.all_to_all(a, "tp", 0, 0)
    groups = [
        [_ctx(y, p >> 1, x + (p & 1), c) for p in range(4)]
        for y in range(NY)
        for x in (0, 2)
        for c in range(NC)
    ]
    return lax.all_to_all(a, "ctx", 0, 0, axis_index_groups=groups)


def _send_tp(a, d):
    return lax.ppermute(a, "tp", [(i, (i + d) % 4) for i in range(4)])


def _pack_body(*refs):
    ins, out, sem = refs[:4], refs[4], refs[5]
    cps = []
    for i, r in enumerate(ins):
        at = out.at[pl.ds(i // 2 * T, r.shape[0]), pl.ds(i % 2 * E, E)]
        cps.append(pltpu.make_async_copy(r, at, sem.at[i]))
    for cp in cps:
        cp.start()
    for cp in cps:
        cp.wait()


def _pack(*arrays):
    return pl.pallas_call(
        _pack_body,
        out_shape=jax.ShapeDtypeStruct((DR, 2 * E), jnp.bfloat16),
        in_specs=[pl.BlockSpec(memory_space=pl.ANY)] * 4,
        out_specs=pl.BlockSpec(memory_space=pltpu.VMEM),
        scratch_shapes=[pltpu.SemaphoreType.DMA((4,))],
        compiler_params=pltpu.CompilerParams(vmem_limit_bytes=60 << 20),
    )(*arrays)


def _flash_body(nb, offs, live, ids, qids, *refs):
    nq = 4
    q_in, refs = refs[:nq], refs[nq:]
    blocks, refs = refs[:nb], refs[nb:]
    out, refs = refs[0], refs[1:]
    qb, kv, m_sc, l_sc, a_sc, *rest = refs
    bufs, (pairs, meta, qsem, sem) = rest[:UN], rest[UN:]
    ntile = kv.shape[0] // TK

    copies = []
    for i in range(nq):
        for h in range(2):
            cp = pltpu.make_async_copy(
                q_in[i].at[:, pl.ds(h * E, E)], qb.at[pl.ds((2 * i + h) * T, T)], qsem.at[2 * i + h]
            )
            cp.start()
            copies.append(cp)
    koff = [offs[ids[j]] for j in range(nb)]
    alive = [live[ids[j // 2] * 2 + j % 2] for j in range(2 * nb)]
    n_live = alive[0]
    for a in alive[1:]:
        n_live = n_live + a
    span0 = n_live * BLK
    dead0 = span0 + nb * T
    seen = jnp.int32(0)
    for j in range(nb):
        rank = jnp.int32(0)
        for i in range(nb):
            if i != j:
                rank = rank + (koff[i] < koff[j]).astype(jnp.int32)
        row = pl.multiple_of(span0 + rank * T, BLK)
        cp = pltpu.make_async_copy(
            blocks[j].at[pl.ds(0, T)], kv.at[pl.ds(row, T)], sem.at[3 * j]
        )
        cp.start()
        copies.append(cp)
        for h in range(2):
            on = alive[2 * j + h]
            row = jnp.where(on > 0, seen * BLK, dead0 + (2 * j + h - seen) * BLK)
            row = pl.multiple_of(row, BLK)
            seen = seen + on
            cp = pltpu.make_async_copy(
                blocks[j].at[pl.ds(T + h * BLK, BLK)], kv.at[pl.ds(row, BLK)], sem.at[3 * j + 1 + h]
            )
            cp.start()
            copies.append(cp)

    n = jnp.int32(0)
    lims = []
    for i in range(nq):
        qid = qids[i]
        before = jnp.int32(0)
        own = jnp.int32(0)
        for j in range(nb):
            before = before + (koff[j] < offs[qid]).astype(jnp.int32)
            own = own + (ids[j] == qid).astype(jnp.int32)
        base = span0 + before * T
        meta[0, i] = base
        meta[1, i] = own
        lims.append((base // TK, pl.cdiv(base + own * T, TK)))

    def listed(i, lo, hi, n):
        def put(t, n):
            pairs[0, n] = i
            pairs[1, n] = t
            return n + 1

        return lax.fori_loop(lo, hi, put, n)

    for i in range(nq):
        n = listed(i, jnp.int32(0), jnp.int32(1), n)
    for i in range(nq):
        n = listed(i, jnp.int32(1), lims[i][0], n)
    clear = (n - nq) // UN
    for i in range(nq):
        n = listed(i, jnp.maximum(lims[i][0], 1), lims[i][1], n)
    rest0 = nq + UN * clear
    rest = pl.cdiv(n - rest0, 2)

    def fill(i, _):
        pairs[0, i] = 0
        pairs[1, i] = ntile
        return 0

    lax.fori_loop(n, rest0 + 2 * rest + 1, fill, 0)
    for cp in copies:
        cp.wait()

    def score(i, dst):
        rows = pl.ds(pl.multiple_of(pairs[0, i] * 2 * T, 2 * T), 2 * T)
        keys = pl.ds(pl.multiple_of(jnp.minimum(pairs[1, i], ntile - 1) * TK, TK), TK)
        dst[...] = lax.dot_general(
            qb[rows, :], kv[keys, :E], (((1,), (1,)), ((), ())), preferred_element_type=jnp.float32
        )

    def absorb(i, src, masked, first=False):
        at, t = pairs[0, i], pairs[1, i]
        rows = pl.ds(pl.multiple_of(at * 2 * T, 2 * T), 2 * T)
        keys = pl.ds(pl.multiple_of(jnp.minimum(t, ntile - 1) * TK, TK), TK)
        s = src[...]
        if masked:
            room = meta[0, at] - t * TK
            tok = lax.rem(lax.broadcasted_iota(jnp.int32, (2 * T, 1), 0), T)
            col = lax.broadcasted_iota(jnp.int32, s.shape, 1)
            s = jnp.where(col < room + meta[1, at] * (tok + 1), s, OUT)
        old = jnp.full((2 * T, 128), LOW, jnp.float32) if first else m_sc[rows]
        new = jnp.maximum(old, jnp.max(s, axis=1, keepdims=True))
        p = jnp.exp2((s - jnp.tile(new, (1, TK // 128))) * C)
        part = p[:, :128]
        for j in range(1, TK // 128):
            part = part + p[:, j * 128 : (j + 1) * 128]
        up = jnp.dot(p.astype(jnp.bfloat16), kv[keys, E:], preferred_element_type=jnp.float32)
        if first:
            l_sc[rows] = part
            a_sc[rows] = up
        else:
            f = jnp.exp2((old - new) * C)
            l_sc[rows] = l_sc[rows] * f + part
            a_sc[rows] = a_sc[rows] * jnp.tile(f, (1, 2)) + up
        m_sc[rows] = new

    def tiles(i, count, **how):
        for u in range(count):
            score(i + u + 1, bufs[(u + 1) % count])
            absorb(i + u, bufs[u], **how)
        return 0

    score(0, bufs[0])
    tiles(0, nq, masked=True, first=True)
    lax.fori_loop(0, clear, lambda j, _: tiles(nq + UN * j, UN, masked=False), 0)
    lax.fori_loop(0, rest, lambda j, _: tiles(rest0 + 2 * j, 2, masked=True), 0)

    lane = lax.broadcasted_iota(jnp.int32, (T, 128), 1)
    for i in range(nq):
        to = ((qids[i] >> 1) & 1) + ((qids[i] >> 2) & 2)
        stats = jnp.zeros((T, 128), jnp.float32)
        for h in range(2):
            rows = pl.ds((2 * i + h) * T, T)
            ls = jnp.sum(l_sc[rows], axis=1, keepdims=True)
            some = ls > 0.0
            safe = jnp.where(some, ls, 1.0)
            o = (a_sc[rows] * (1.0 / safe)).astype(jnp.bfloat16)
            lse = jnp.where(some, m_sc[rows] * C + jnp.log2(safe), LOW)
            hi = lse.astype(jnp.bfloat16).astype(jnp.float32)
            mid = (lse - hi).astype(jnp.bfloat16).astype(jnp.float32)
            lo = lse - hi - mid
            for k, x in enumerate((hi, mid, lo)):
                stats = jnp.where(lane == h * 8 + k, x, stats)
            out[to, :T, h * E : (h + 1) * E] = o
        out[to, T:, :T] = stats.T[:ST].astype(jnp.bfloat16)
        out[to, T:, T:] = jnp.zeros((ST, 2 * E - T), jnp.bfloat16)


def _flash(offs, live, ids, qids, qs, blocks):
    nb, nq = len(blocks), len(qs)
    rows = nq * 2 * T
    keys = nb * (T + CB)
    return pl.pallas_call(
        functools.partial(_flash_body, nb),
        out_shape=jax.ShapeDtypeStruct((nq, T + ST, 2 * E), jnp.bfloat16),
        grid_spec=pltpu.PrefetchScalarGridSpec(
            num_scalar_prefetch=4,
            grid=(1,),
            in_specs=[pl.BlockSpec(memory_space=pltpu.HBM)] * (nq + nb),
            out_specs=pl.BlockSpec(memory_space=pltpu.VMEM),
            scratch_shapes=[
                pltpu.VMEM((rows, E), jnp.bfloat16),
                pltpu.VMEM((keys, 2 * E), jnp.bfloat16),
                pltpu.VMEM((rows, 128), jnp.float32),
                pltpu.VMEM((rows, 128), jnp.float32),
                pltpu.VMEM((rows, E), jnp.float32),
                *[pltpu.VMEM((2 * T, TK), jnp.float32)] * UN,
                pltpu.SMEM((2, 128), jnp.int32),
                pltpu.SMEM((2, 8), jnp.int32),
                pltpu.SemaphoreType.DMA((2 * nq,)),
                pltpu.SemaphoreType.DMA((3 * nb,)),
            ],
        ),
        compiler_params=pltpu.CompilerParams(vmem_limit_bytes=60 << 20),
        cost_estimate=pl.CostEstimate(
            flops=rows * keys * E * 4 * 6 // 10,
            bytes_accessed=keys * E * 4 + rows * E * 6,
            transcendentals=rows * keys * 6 // 10,
        ),
    )(offs, live, ids, qids, *qs, *blocks)


def _merge_body(parts, top, bottom):
    lses = []
    for i in range(4):
        flat = parts[i, T:, :T].astype(jnp.float32)
        lses.append(jnp.concatenate([flat, jnp.zeros((128 - ST, T), jnp.float32)], axis=0).T)
    for h in range(2):
        k = h * 8
        ls = [s[:, k : k + 1] + s[:, k + 1 : k + 2] + s[:, k + 2 : k + 3] for s in lses]
        peak = functools.reduce(jnp.maximum, ls)
        ws = [jnp.exp2(x - peak) for x in ls]
        inv = 1.0 / functools.reduce(jnp.add, ws)
        o = 0.0
        for i, w in enumerate(ws):
            o = o + parts[i, :T, h * E : (h + 1) * E].astype(jnp.float32) * (w * inv)
        o = o.astype(jnp.bfloat16)
        top[:, h * E : (h + 1) * E] = o[:H]
        bottom[:, h * E : (h + 1) * E] = o[H:]


def _merge(parts):
    return pl.pallas_call(
        _merge_body,
        out_shape=[jax.ShapeDtypeStruct((H, 2 * E), jnp.bfloat16)] * 2,
        in_specs=[pl.BlockSpec(memory_space=pltpu.VMEM)],
        out_specs=[pl.BlockSpec(memory_space=pltpu.VMEM)] * 2,
        compiler_params=pltpu.CompilerParams(vmem_limit_bytes=6 << 20),
        cost_estimate=pl.CostEstimate(
            flops=4 * T * E * 8, bytes_accessed=4 * T * E * 6, transcendentals=T * 16
        ),
    )(parts)


def _weave_body(n, pos, *refs):
    pieces, outs, sem = refs[:n], refs[n : n + 3], refs[n + 3]
    cps = []
    for i in range(n):
        rows = pieces[i].shape[1]
        at = pl.ds(pl.multiple_of(pos[i], rows), rows)
        for d in range(3):
            cps.append(pltpu.make_async_copy(pieces[i].at[d], outs[d].at[at], sem.at[3 * i + d]))
    for cp in cps:
        cp.start()
    for cp in cps:
        cp.wait()


def _weave(pos, pieces):
    n, (_, rows, width) = len(pieces), pieces[0].shape
    return pl.pallas_call(
        functools.partial(_weave_body, n),
        out_shape=[jax.ShapeDtypeStruct((n * rows, width), jnp.bfloat16)] * 3,
        grid_spec=pltpu.PrefetchScalarGridSpec(
            num_scalar_prefetch=1,
            grid=(1,),
            in_specs=[pl.BlockSpec(memory_space=pltpu.HBM)] * n,
            out_specs=[pl.BlockSpec(memory_space=pltpu.VMEM)] * 3,
            scratch_shapes=[pltpu.SemaphoreType.DMA((3 * n,))],
        ),
        compiler_params=pltpu.CompilerParams(vmem_limit_bytes=12 << 20),
    )(pos, *pieces)


def _project(ws, xs, acc, last):
    n, cols = len(ws), ws[0].shape[1]
    flat = [h for x in xs for h in x]

    def body(*refs):
        wr, xr, rest = refs[:n], list(refs[n : n + len(flat)]), refs[n + len(flat) :]
        out = rest[-1]
        for g in range(2):
            at = slice(g * H, (g + 1) * H)
            k, total = 0, None if acc is None else rest[0][at, :]
            for w, x in zip(wr, xs):
                rows = xr[k][at, :] if len(x) == 1 else xr[k + g][...]
                k += len(x)
                y = jnp.dot(rows, w[...], preferred_element_type=jnp.float32)
                total = y if total is None else total + y
            out[at, :] = total.astype(out.dtype)

    args = list(ws) + flat + ([] if acc is None else [acc])
    return pl.pallas_call(
        body,
        out_shape=jax.ShapeDtypeStruct((T, cols), jnp.bfloat16 if last else jnp.float32),
        in_specs=[pl.BlockSpec(memory_space=pltpu.VMEM)] * len(args),
        out_specs=pl.BlockSpec(memory_space=pltpu.VMEM),
        compiler_params=pltpu.CompilerParams(vmem_limit_bytes=12 << 20),
        cost_estimate=pl.CostEstimate(
            flops=n * 2 * T * 2 * E * cols,
            bytes_accessed=n * 4 * E * cols + 8 * T * cols,
            transcendentals=0,
        ),
    )(*args)


def _tables(me, earlier_block_slot, prior_block_count):
    y, z, x, c = me >> 4, (me >> 3) & 1, (me >> 1) & 3, me & 1
    steps = [(0, 0), (0, 3), (-1, 0), (1, 0), (-1, 3), (1, 3), (2, 0), (2, 3)]
    flip = [(dy, fx, fc) for fc in (0, 1) for dy, fx in steps]
    dy, fx, fc = (jnp.array(a, jnp.int32) for a in zip(*flip))
    ids = (((y + dy) & 3) << 4) + (z << 3) + ((x ^ fx) << 1) + (c ^ fc)
    qids = me ^ jnp.array([0, 2, 8, 10], jnp.int32)
    slots = jnp.arange(earlier_block_slot.shape[0], dtype=jnp.int32)
    hit = (earlier_block_slot[None, :] == slots[:, None]) & (slots[None, :] < prior_block_count[0])
    return ids, qids, jnp.sum(hit.astype(jnp.int32), axis=1)


def per_device(
    queries,
    span_keys,
    span_values,
    cache_keys,
    cache_values,
    out_weight,
    offsets,
    earlier_block_slot,
    prior_block_count,
):
    me = lax.axis_index("ctx")
    tp = lax.axis_index("tp")
    y, c = me >> 4, me & 1

    cols = out_weight.shape[1] // 4
    part = out_weight.shape[0] // 8
    cut = lax.dynamic_slice_in_dim(out_weight, (y * NC + c) * part, part, 0)
    cut = cut.reshape(part, 4, cols).transpose(1, 0, 2)

    d0 = _pack(span_keys, span_values, cache_keys, cache_values)
    e0 = _send(d0, fx=3)
    dm = _send(d0, dy=1)
    dp = _send(d0, dy=-1)
    cd0 = _send(d0, fc=1)
    tables = (*_tables(me, earlier_block_slot, prior_block_count), cut)
    e0, tables = lax.optimization_barrier((e0, tables))
    ids, qids, live, cut = tables
    q3 = _send(queries, fz=1, fx=1)
    q1 = _send(queries, fx=1)
    q2 = _send(queries, fz=1)
    em = _send(e0, dy=1)
    ep = _send(e0, dy=-1)
    ce0 = _send(e0, fc=1)
    d2 = _send(dm, dy=1)
    cdm = _send(dm, fc=1)
    cdp = _send(dp, fc=1)
    e2 = _send(ep, dy=-1)
    cem = _send(em, fc=1)
    cep = _send(ep, fc=1)
    cd2 = _send(d2, fc=1)
    ce2 = _send(e2, fc=1)
    blocks = [d0, e0, dm, dp, em, ep, d2, e2, cd0, ce0, cdm, cdp, cem, cep, cd2, ce2]
    wt = _swap(cut, "tp")
    turn = jnp.array([0, -1, 1, 2], jnp.int32)
    row = ((y + turn) & 3) * (NC * part)
    pos = jnp.concatenate([row + c * part, row + (c ^ 1) * part]).astype(jnp.int32)
    parts = _flash(offsets, live, ids, qids, [queries, q1, q2, q3], blocks)
    wt = jnp.stack([lax.dynamic_index_in_dim(wt, (tp + d) & 3, 0, False) for d in (3, 1, 2)])
    pieces = [wt, _send(wt, dy=1), _send(wt, dy=-1), _send(wt, dy=2)]
    pieces = pieces + [_send(w, fc=1) for w in pieces]
    wm, wp, w2 = _weave(pos, pieces)
    weight, parts = lax.optimization_barrier((out_weight, parts))
    w0 = lax.dynamic_slice_in_dim(weight, tp * cols, cols, 1)

    top, bottom = _merge(_swap(parts, "x"))
    tm, bq = _send_tp(top, 1), _send_tp(bottom, 3)
    tq, bm = _send_tp(top, 3), _send_tp(bottom, 1)
    t2, b2 = _send_tp(tm, 1), _send_tp(bq, 3)
    acc = _project([w0, wm, wp], [[top, bottom], [tm, bm], [tq, bq]], None, False)
    return _project([w2], [[t2, b2]], acc, True)


def solution(mesh):
    placed = (
        P("ctx", "tp"),
        P("ctx", "tp"),
        P("ctx", "tp"),
        P("ctx", "tp"),
        P("ctx", "tp"),
        P("tp", None),
        P(),
        P(),
        P(),
    )

    return jax.shard_map(
        per_device, mesh=mesh, in_specs=placed, out_specs=P("ctx", "tp"), check_vma=False
    )
```

time: 532 us -> 136 us (0.26)
  the two profiles are of different devices: /device:TPU:1 before, /device:TPU:58 now
where the time goes in v1:
time: 136 us; the launch traced here: 135 us
  waiting for transfers between devices  51.3 us (38%)
  starting transfers between devices  39 us (29%)
  Pallas kernels  34.1 us (25%)
  local copies, waits for them, and re-layouts  6 us (4%)
  other arithmetic  3.86 us (3%)
    ppermute x25, waiting for transfers between devices, _send(): return lax.ppermute(a, 'ctx', pairs)  44.8 us
    pallas_call x1, Pallas kernels, _flash(): pl.pallas_call(functools.partial(_flash_body, nb), out_shape=jax.ShapeDty...  23.5 us
    ppermute x25, starting transfers between devices, _send(): return lax.ppermute(a, 'ctx', pairs)  14.8 us
    ppermute x6, starting transfers between devices, _send_tp(): return lax.ppermute(a, 'tp', [(i, (i + d) % 4) for i in range(4)])  12.4 us
    all_to_all x1, starting transfers between devices, _swap(): return lax.all_to_all(a, 'tp', 0, 0)  7.56 us
    ppermute x6, waiting for transfers between devices, _send_tp(): return lax.ppermute(a, 'tp', [(i, (i + d) % 4) for i in range(4)])  6.52 us
    pallas_call x1, Pallas kernels, _weave(): pl.pallas_call(functools.partial(_weave_body, n), out_shape=[jax.ShapeDty...  5.01 us
    all_to_all x1, starting transfers between devices, _swap(): return lax.all_to_all(a, 'ctx', 0, 0, axis_index_groups=groups)  4.2 us
  transfers between devices with their start and end apart: 33, of which 7 were waited for; matrix products, arithmetic and copies ran while one was open for 6% of the time, Pallas kernels for 24%

profile of v1, /device:TPU:58, one launch (start us, length us, event | category | flops | bytes accessed | tf_op | source)
XLA Modules:
  0.0 135.3 jit_solution(8806882044593770847)
XLA Ops:
  0.0 1.8 %shard_map.136.refs_4_ = bf16[384,512]{1,0:T(8,128)(2,1)} custom-call(bf16[256,256]{1,0:T(8,128)(2,1)} %refs_0_.2, bf16[256,256]{1,0:T(8,128)(2,1)} %refs_1_.1, bf16[128,256]{1,0:T(8,128)(2,1)} %refs_2_.1, bf16[128,256]{1,0:T(8,128)(2,1)} %refs_3_.1), custom_call_target="tpu_custom_call" | custom-call | tf_op jit(solution)/shard_map/pallas_call | solution.py:71
  1.8 1.6 %collective-permute-start = (bf16[384,512]{1,0:T(8,128)(2,1)}, bf16[384,512]{1,0:T(8,128)(2,1)S(1)}, u32[]{:S(2)}, u32[]{:S(2)}) collective-permute-start(bf16[384,512]{1,0:T(8,128)(2,1)} %shard_map.136.refs_4_), channel_id=1, source_target_pairs={{0,24},{4,28},{8,16},{12,20},{16,8},{20,12},{24,0},{28,4},{32,56},... | collective-permute-start | bytes 1179656 | tf_op jit(solution)/shard_map/ppermute | solution.py:39
  3.6 1.8 %collective-permute-start.12 = (bf16[384,512]{1,0:T(8,128)(2,1)}, bf16[384,512]{1,0:T(8,128)(2,1)S(1)}, u32[]{:S(2)}, u32[]{:S(2)}) collective-permute-start(bf16[384,512]{1,0:T(8,128)(2,1)} %shard_map.136.refs_4_), channel_id=1, source_target_pairs={{0,192},{4,196},{8,200},{12,204},{16,208},{20,212},{24,216},{28,22... | collective-permute-start | bytes 1179656 | tf_op jit(solution)/shard_map/ppermute | solution.py:39
  5.4 1.3 collective-permute-start.10
  7.2 1.1 constant_dynamic-slice_fusion.4
  8.3 1.3 xor_add_fusion.ids
  9.5 1.2 broadcast_xor_fusion.qids
  12.1 1.0 copy.21
  13.1 1.2 convert_reduce_fusion.live
  15.2 4.2 %collective-permute-done.8.refs_1_ = bf16[256,512]{1,0:T(8,128)(2,1)S(1)} collective-permute-done((bf16[256,512]{1,0:T(8,128)(2,1)}, bf16[256,512]{1,0:T(8,128)(2,1)S(1)}, u32[]{:S(2)}, u32[]{:S(2)}) %collective-permute-start.8) | collective-permute-done | bytes 262176 | tf_op jit(solution)/shard_map/ppermute | solution.py:39
  20.0 7.7 %collective-permute-done.9.refs_2_ = bf16[256,512]{1,0:T(8,128)(2,1)S(1)} collective-permute-done((bf16[256,512]{1,0:T(8,128)(2,1)}, bf16[256,512]{1,0:T(8,128)(2,1)S(1)}, u32[]{:S(2)}, u32[]{:S(2)}) %collective-permute-start.9) | collective-permute-done | bytes 262176 | tf_op jit(solution)/shard_map/ppermute | solution.py:39
  27.8 1.5 %collective-permute-start.13 = (bf16[384,512]{1,0:T(8,128)(2,1)S(1)}, bf16[384,512]{1,0:T(8,128)(2,1)S(1)}, u32[]{:S(2)}, u32[]{:S(2)}) collective-permute-start(bf16[384,512]{1,0:T(8,128)(2,1)S(1)} %collective-permute-done.refs_5_), channel_id=1, source_target_pairs={{0,64},{4,68},{8,72},{12,76},{16,80},{20,84},{24,88},{28,92},{32,9... | collective-permute-start | bytes 1179656 | tf_op jit(solution)/shard_map/ppermute | solution.py:39
  29.9 1.7 %collective-permute-start.16 = (bf16[384,512]{1,0:T(8,128)(2,1)S(1)}, bf16[384,512]{1,0:T(8,128)(2,1)}, u32[]{:S(2)}, u32[]{:S(2)}) collective-permute-start(bf16[384,512]{1,0:T(8,128)(2,1)S(1)} %collective-permute-done.14.refs_9_), channel_id=1, source_target_pairs={{0,192},{4,196},{8,200},{12,204},{16,208},{20,212},{24,216},{28,22... | collective-permute-start | bytes 1179656 | tf_op jit(solution)/shard_map/ppermute | solution.py:39
  31.6 8.1 %collective-permute-done.13.refs_8_ = bf16[384,512]{1,0:T(8,128)(2,1)S(1)} collective-permute-done((bf16[384,512]{1,0:T(8,128)(2,1)S(1)}, bf16[384,512]{1,0:T(8,128)(2,1)S(1)}, u32[]{:S(2)}, u32[]{:S(2)}) %collective-permute-start.13) | collective-permute-done | bytes 393248 | tf_op jit(solution)/shard_map/ppermute | solution.py:39
  40.3 6.2 %collective-permute-done.15.refs_10_ = bf16[384,512]{1,0:T(8,128)(2,1)} collective-permute-done((bf16[384,512]{1,0:T(8,128)(2,1)S(1)}, bf16[384,512]{1,0:T(8,128)(2,1)}, u32[]{:S(2)}, u32[]{:S(2)}) %collective-permute-start.15) | collective-permute-done | bytes 393248 | tf_op jit(solution)/shard_map/ppermute | solution.py:39
  47.7 7.6 %all-to-all-start = ((bf16[4,64,960]{2,1,0:T(8,128)(2,1)}), bf16[4,64,960]{2,1,0:T(8,128)(2,1)S(1)}, u32[]{:S(2)}, u32[]{:S(2)}) async-start(bf16[4,64,960]{2,1,0:T(8,128)(2,1)} %bitcast.3), calls=%async_computation | async-start | bytes 1048576 | tf_op jit(solution)/shard_map/all_to_all | solution.py:44
  55.4 23.5 %shard_map.138 = bf16[4,272,512]{2,1,0:T(8,128)(2,1)} custom-call(s32[64]{0:T(128)} %offs.1, s32[128]{0:T(128)} %convert_reduce_fusion.live, s32[16]{0:T(128)} %xor_add_fusion.ids, s32[4]{0:T(128)} %broadcast_xor_fusion.qids, bf16[256,512]{1,0:T(8,128)(2,1)} %refs_0_.3, bf16[256,512]{1,0:T(8,128)(2,1)} %copy-done.9, bf16[256,512]{1,0:T(8,128)(2,1)} %copy-done.10, ...), custom_call_target="tpu_custom_call" | custom-call | flops 7730940928 | bytes 9437184 | tf_op jit(solution)/shard_map/pallas_call | solution.py:238
  78.9 4.2 %all-to-all-start.1 = ((bf16[4,272,512]{2,1,0:T(8,128)(2,1)}), bf16[4,272,512]{2,1,0:T(8,128)(2,1)S(1)}, u32[]{:S(2)}, u32[]{:S(2)}) async-start(bf16[4,272,512]{2,1,0:T(8,128)(2,1)} %shard_map.138), calls=%async_computation.1 | async-start | bytes 2228224 | tf_op jit(solution)/shard_map/all_to_all | solution.py:51
  83.3 2.0 %collective-permute-start.2 = (bf16[3,64,960]{2,1,0:T(8,128)(2,1)S(1)}, bf16[3,64,960]{2,1,0:T(8,128)(2,1)S(1)}, u32[]{:S(2)}, u32[]{:S(2)}) collective-permute-start(bf16[3,64,960]{2,1,0:T(8,128)(2,1)S(1)} %pad_maximum_fusion.refs_0_), channel_id=1, source_target_pairs={{0,192},{4,196},{8,200},{12,204},{16,208},{20,212},{24,216},{28,22... | collective-permute-start | bytes 1105928 | tf_op jit(solution)/shard_map/ppermute | solution.py:39
  85.3 15.2 %collective-permute-done.1.refs_1_ = bf16[3,64,960]{2,1,0:T(8,128)(2,1)S(1)} collective-permute-done((bf16[3,64,960]{2,1,0:T(8,128)(2,1)S(1)}, bf16[3,64,960]{2,1,0:T(8,128)(2,1)S(1)}, u32[]{:S(2)}, u32[]{:S(2)}) %collective-permute-start.1) | collective-permute-done | bytes 368672 | tf_op jit(solution)/shard_map/ppermute | solution.py:39
  100.5 3.4 %collective-permute-done.2.refs_2_ = bf16[3,64,960]{2,1,0:T(8,128)(2,1)S(1)} collective-permute-done((bf16[3,64,960]{2,1,0:T(8,128)(2,1)S(1)}, bf16[3,64,960]{2,1,0:T(8,128)(2,1)S(1)}, u32[]{:S(2)}, u32[]{:S(2)}) %collective-permute-start.2) | collective-permute-done | bytes 368672 | tf_op jit(solution)/shard_map/ppermute | solution.py:39
  104.4 1.4 %shard_map.139 = (bf16[128,512]{1,0:T(8,128)(2,1)}, bf16[128,512]{1,0:T(8,128)(2,1)}) custom-call(bf16[4,272,512]{2,1,0:T(8,128)(2,1)S(1)} %all-to-all-done.1.parts), custom_call_target="tpu_custom_call" | custom-call | flops 2097152 | bytes 1572864 | tf_op jit(solution)/shard_map/pallas_call | solution.py:288
  105.8 2.6 %collective-permute-start.25 = (bf16[128,512]{1,0:T(8,128)(2,1)}, bf16[128,512]{1,0:T(8,128)(2,1)S(1)}, u32[]{:S(2)}, u32[]{:S(2)}) collective-permute-start(bf16[128,512]{1,0:T(8,128)(2,1)} %get-tuple-element.24.refs_3_), channel_id=1, source_target_pairs={{0,1},{1,2},{2,3},{3,0},{4,5},{5,6},{6,7},{7,4},{8,9},{9,10},{10,1... | collective-permute-start | bytes 393224 | tf_op jit(solution)/shard_map/ppermute | solution.py:55
  108.5 1.5 %collective-permute-start.27 = (bf16[128,512]{1,0:T(8,128)(2,1)}, bf16[128,512]{1,0:T(8,128)(2,1)S(1)}, u32[]{:S(2)}, u32[]{:S(2)}) collective-permute-start(bf16[128,512]{1,0:T(8,128)(2,1)} %get-tuple-element.25.refs_4_), channel_id=1, source_target_pairs={{0,3},{1,0},{2,1},{3,2},{4,7},{5,4},{6,5},{7,6},{8,11},{9,8},{10,9... | collective-permute-start | bytes 393224 | tf_op jit(solution)/shard_map/ppermute | solution.py:55
  110.1 2.1 %collective-permute-start.29 = (bf16[128,512]{1,0:T(8,128)(2,1)}, bf16[128,512]{1,0:T(8,128)(2,1)S(1)}, u32[]{:S(2)}, u32[]{:S(2)}) collective-permute-start(bf16[128,512]{1,0:T(8,128)(2,1)} %get-tuple-element.25.refs_4_), channel_id=1, source_target_pairs={{0,1},{1,2},{2,3},{3,0},{4,5},{5,6},{6,7},{7,4},{8,9},{9,10},{10,1... | collective-permute-start | bytes 393224 | tf_op jit(solution)/shard_map/ppermute | solution.py:55
  112.2 2.0 %collective-permute-start.30 = (bf16[128,512]{1,0:T(8,128)(2,1)}, bf16[128,512]{1,0:T(8,128)(2,1)S(1)}, u32[]{:S(2)}, u32[]{:S(2)}) collective-permute-start(bf16[128,512]{1,0:T(8,128)(2,1)} %get-tuple-element.24.refs_3_), channel_id=1, source_target_pairs={{0,3},{1,0},{2,1},{3,2},{4,7},{5,4},{6,5},{7,6},{8,11},{9,8},{10,9... | collective-permute-start | bytes 393224 | tf_op jit(solution)/shard_map/ppermute | solution.py:55
  114.2 6.5 %collective-permute-done.25.refs_5_ = bf16[128,512]{1,0:T(8,128)(2,1)S(1)} collective-permute-done((bf16[128,512]{1,0:T(8,128)(2,1)}, bf16[128,512]{1,0:T(8,128)(2,1)S(1)}, u32[]{:S(2)}, u32[]{:S(2)}) %collective-permute-start.25) | collective-permute-done | bytes 131104 | tf_op jit(solution)/shard_map/ppermute | solution.py:55
  121.3 3.6 %collective-permute-start.28 = (bf16[128,512]{1,0:T(8,128)(2,1)S(1)}, bf16[128,512]{1,0:T(8,128)(2,1)S(1)}, u32[]{:S(2)}, u32[]{:S(2)}) collective-permute-start(bf16[128,512]{1,0:T(8,128)(2,1)S(1)} %collective-permute-done.27.refs_8_), channel_id=1, source_target_pairs={{0,3},{1,0},{2,1},{3,2},{4,7},{5,4},{6,5},{7,6},{8,11},{9,8},{10,9... | collective-permute-start | bytes 393224 | tf_op jit(solution)/shard_map/ppermute | solution.py:55
  124.9 1.9 %constant_dynamic-slice_fusion.refs_0_ = bf16[512,960]{1,0:T(8,128)(2,1)S(1)} fusion(bf16[512,3840]{1,0:T(8,128)(2,1)} %param.19, s32[]{:T(128)S(6)} %select_n.20), kind=kLoop, calls=%fused_computation.5 | loop fusion | bytes 1966084 | tf_op jit(solution)/shard_map/dynamic_slice | solution.py:427
  126.8 5.0 %shard_map.137 = (bf16[512,960]{1,0:T(8,128)(2,1)S(1)}, bf16[512,960]{1,0:T(8,128)(2,1)S(1)}, bf16[512,960]{1,0:T(8,128)(2,1)S(1)}) custom-call(s32[8]{0:T(128)S(1)} %pad_add_fusion.pos, bf16[3,64,960]{2,1,0:T(8,128)(2,1)S(1)} %pad_maximum_fusion.refs_0_, bf16[3,64,960]{2,1,0:T(8,128)(2,1)S(1)} %collective-permute-done.1.refs_1_, ...), custom_call_target="tpu_custom_call" | custom-call | tf_op jit(solution)/shard_map/pallas_call | solution.py:316
  131.8 2.0 %shard_map.140.refs_3_ = f32[256,960]{1,0:T(8,128)S(1)} custom-call(bf16[512,960]{1,0:T(8,128)(2,1)S(1)} %constant_dynamic-slice_fusion.refs_0_, bf16[512,960]{1,0:T(8,128)(2,1)S(1)} %get-tuple-element.27.refs_1_, bf16[512,960]{1,0:T(8,128)(2,1)S(1)} %get-tuple-element.28.refs_2_, bf16[128,512]{1,0:T(8,128)(2,1)} %get-tuple-element.24.refs_3_, ...), custom_call_target="tpu_custom_call" | custom-call | flops 754974720 | bytes 4915200 | tf_op jit(solution)/shard_map/pallas_call | solution.py:348
  134.3 1.0 copy.19
  (75 shorter events, 7.2 us)
Async XLA Ops:
  1.8 12.6 %collective-permute-start = (bf16[384,512]{1,0:T(8,128)(2,1)}, bf16[384,512]{1,0:T(8,128)(2,1)S(1)}, u32[]{:S(2)}, u32[]{:S(2)}) collective-permute-start(bf16[384,512]{1,0:T(8,128)(2,1)} %shard_map.136.refs_4_), channel_id=1, source_target_pairs={{0,24},{4,28},{8,16},{12,20},{16,8},{20,12},{24,0},{28,4},{32,56},... | collective-permute-start | bytes 1179656 | tf_op jit(solution)/shard_map/ppermute | solution.py:39
  3.4 25.9 %collective-permute-start.11 = (bf16[384,512]{1,0:T(8,128)(2,1)}, bf16[384,512]{1,0:T(8,128)(2,1)S(1)}, u32[]{:S(2)}, u32[]{:S(2)}) collective-permute-start(bf16[384,512]{1,0:T(8,128)(2,1)} %shard_map.136.refs_4_), channel_id=1, source_target_pairs={{0,64},{4,68},{8,72},{12,76},{16,80},{20,84},{24,88},{28,92},{32,9... | collective-permute-start | bytes 1179656 | tf_op jit(solution)/shard_map/ppermute | solution.py:39
  3.6 25.7 %collective-permute-start.12 = (bf16[384,512]{1,0:T(8,128)(2,1)}, bf16[384,512]{1,0:T(8,128)(2,1)S(1)}, u32[]{:S(2)}, u32[]{:S(2)}) collective-permute-start(bf16[384,512]{1,0:T(8,128)(2,1)} %shard_map.136.refs_4_), channel_id=1, source_target_pairs={{0,192},{4,196},{8,200},{12,204},{16,208},{20,212},{24,216},{28,22... | collective-permute-start | bytes 1179656 | tf_op jit(solution)/shard_map/ppermute | solution.py:39
  5.4 9.0 %collective-permute-start.10 = (bf16[256,512]{1,0:T(8,128)(2,1)}, bf16[256,512]{1,0:T(8,128)(2,1)}, u32[]{:S(2)}, u32[]{:S(2)}) collective-permute-start(bf16[256,512]{1,0:T(8,128)(2,1)} %refs_0_.3), channel_id=1, source_target_pairs={{0,40},{4,44},{8,32},{12,36},{16,56},{20,60},{24,48},{28,52},{32,8... | collective-permute-start | bytes 786440 | tf_op jit(solution)/shard_map/ppermute | solution.py:39
  6.7 12.6 %collective-permute-start.8 = (bf16[256,512]{1,0:T(8,128)(2,1)}, bf16[256,512]{1,0:T(8,128)(2,1)S(1)}, u32[]{:S(2)}, u32[]{:S(2)}) collective-permute-start(bf16[256,512]{1,0:T(8,128)(2,1)} %refs_0_.3), channel_id=1, source_target_pairs={{0,8},{4,12},{8,0},{12,4},{16,24},{20,28},{24,16},{28,20},{32,40},... | collective-permute-start | bytes 786440 | tf_op jit(solution)/shard_map/ppermute | solution.py:39
  14.3 15.3 %collective-permute-start.17 = (bf16[384,512]{1,0:T(8,128)(2,1)}, bf16[384,512]{1,0:T(8,128)(2,1)S(1)}, u32[]{:S(2)}, u32[]{:S(2)}) collective-permute-start(bf16[384,512]{1,0:T(8,128)(2,1)} %shard_map.136.refs_4_), channel_id=1, source_target_pairs={{0,4},{4,0},{8,12},{12,8},{16,20},{20,16},{24,28},{28,24},{32,36},... | collective-permute-start | bytes 1179656 | tf_op jit(solution)/shard_map/ppermute | solution.py:39
  14.3 15.6 %collective-permute-start.14 = (bf16[384,512]{1,0:T(8,128)(2,1)S(1)}, bf16[384,512]{1,0:T(8,128)(2,1)S(1)}, u32[]{:S(2)}, u32[]{:S(2)}) collective-permute-start(bf16[384,512]{1,0:T(8,128)(2,1)S(1)} %collective-permute-done.refs_5_), channel_id=1, source_target_pairs={{0,192},{4,196},{8,200},{12,204},{16,208},{20,212},{24,216},{28,22... | collective-permute-start | bytes 1179656 | tf_op jit(solution)/shard_map/ppermute | solution.py:39
  19.3 8.4 %collective-permute-start.9 = (bf16[256,512]{1,0:T(8,128)(2,1)}, bf16[256,512]{1,0:T(8,128)(2,1)S(1)}, u32[]{:S(2)}, u32[]{:S(2)}) collective-permute-start(bf16[256,512]{1,0:T(8,128)(2,1)} %refs_0_.3), channel_id=1, source_target_pairs={{0,32},{4,36},{8,40},{12,44},{16,48},{20,52},{24,56},{28,60},{32,0... | collective-permute-start | bytes 786440 | tf_op jit(solution)/shard_map/ppermute | solution.py:39
  27.8 12.0 %collective-permute-start.13 = (bf16[384,512]{1,0:T(8,128)(2,1)S(1)}, bf16[384,512]{1,0:T(8,128)(2,1)S(1)}, u32[]{:S(2)}, u32[]{:S(2)}) collective-permute-start(bf16[384,512]{1,0:T(8,128)(2,1)S(1)} %collective-permute-done.refs_5_), channel_id=1, source_target_pairs={{0,64},{4,68},{8,72},{12,76},{16,80},{20,84},{24,88},{28,92},{32,9... | collective-permute-start | bytes 1179656 | tf_op jit(solution)/shard_map/ppermute | solution.py:39
  29.3 10.5 %collective-permute-start.18 = (bf16[384,512]{1,0:T(8,128)(2,1)S(1)}, bf16[384,512]{1,0:T(8,128)(2,1)S(1)}, u32[]{:S(2)}, u32[]{:S(2)}) collective-permute-start(bf16[384,512]{1,0:T(8,128)(2,1)S(1)} %collective-permute-done.refs_5_), channel_id=1, source_target_pairs={{0,4},{4,0},{8,12},{12,8},{16,20},{20,16},{24,28},{28,24},{32,36},... | collective-permute-start | bytes 1179656 | tf_op jit(solution)/shard_map/ppermute | solution.py:39
  29.3 17.2 %collective-permute-start.15 = (bf16[384,512]{1,0:T(8,128)(2,1)S(1)}, bf16[384,512]{1,0:T(8,128)(2,1)}, u32[]{:S(2)}, u32[]{:S(2)}) collective-permute-start(bf16[384,512]{1,0:T(8,128)(2,1)S(1)} %collective-permute-done.11.refs_6_), channel_id=1, source_target_pairs={{0,64},{4,68},{8,72},{12,76},{16,80},{20,84},{24,88},{28,92},{32,9... | collective-permute-start | bytes 1179656 | tf_op jit(solution)/shard_map/ppermute | solution.py:39
  29.7 16.8 %collective-permute-start.19 = (bf16[384,512]{1,0:T(8,128)(2,1)S(1)}, bf16[384,512]{1,0:T(8,128)(2,1)S(1)}, u32[]{:S(2)}, u32[]{:S(2)}) collective-permute-start(bf16[384,512]{1,0:T(8,128)(2,1)S(1)} %collective-permute-done.11.refs_6_), channel_id=1, source_target_pairs={{0,4},{4,0},{8,12},{12,8},{16,20},{20,16},{24,28},{28,24},{32,36},... | collective-permute-start | bytes 1179656 | tf_op jit(solution)/shard_map/ppermute | solution.py:39
  29.9 17.1 %collective-permute-start.16 = (bf16[384,512]{1,0:T(8,128)(2,1)S(1)}, bf16[384,512]{1,0:T(8,128)(2,1)}, u32[]{:S(2)}, u32[]{:S(2)}) collective-permute-start(bf16[384,512]{1,0:T(8,128)(2,1)S(1)} %collective-permute-done.14.refs_9_), channel_id=1, source_target_pairs={{0,192},{4,196},{8,200},{12,204},{16,208},{20,212},{24,216},{28,22... | collective-permute-start | bytes 1179656 | tf_op jit(solution)/shard_map/ppermute | solution.py:39
  39.8 15.5 %collective-permute-start.20 = (bf16[384,512]{1,0:T(8,128)(2,1)S(1)}, bf16[384,512]{1,0:T(8,128)(2,1)}, u32[]{:S(2)}, u32[]{:S(2)}) collective-permute-start(bf16[384,512]{1,0:T(8,128)(2,1)S(1)} %collective-permute-done.12.refs_7_), channel_id=1, source_target_pairs={{0,4},{4,0},{8,12},{12,8},{16,20},{20,16},{24,28},{28,24},{32,36},... | collective-permute-start | bytes 1179656 | tf_op jit(solution)/shard_map/ppermute | solution.py:39
  39.8 15.5 %collective-permute-start.22 = (bf16[384,512]{1,0:T(8,128)(2,1)S(1)}, bf16[384,512]{1,0:T(8,128)(2,1)}, u32[]{:S(2)}, u32[]{:S(2)}) collective-permute-start(bf16[384,512]{1,0:T(8,128)(2,1)S(1)} %collective-permute-done.14.refs_9_), channel_id=1, source_target_pairs={{0,4},{4,0},{8,12},{12,8},{16,20},{20,16},{24,28},{28,24},{32,36},... | collective-permute-start | bytes 1179656 | tf_op jit(solution)/shard_map/ppermute | solution.py:39
  46.5 8.8 %collective-permute-start.21 = (bf16[384,512]{1,0:T(8,128)(2,1)S(1)}, bf16[384,512]{1,0:T(8,128)(2,1)}, u32[]{:S(2)}, u32[]{:S(2)}) collective-permute-start(bf16[384,512]{1,0:T(8,128)(2,1)S(1)} %collective-permute-done.13.refs_8_), channel_id=1, source_target_pairs={{0,4},{4,0},{8,12},{12,8},{16,20},{20,16},{24,28},{28,24},{32,36},... | collective-permute-start | bytes 1179656 | tf_op jit(solution)/shard_map/ppermute | solution.py:39
  46.5 8.8 %collective-permute-start.23 = (bf16[384,512]{1,0:T(8,128)(2,1)}, bf16[384,512]{1,0:T(8,128)(2,1)}, u32[]{:S(2)}, u32[]{:S(2)}) collective-permute-start(bf16[384,512]{1,0:T(8,128)(2,1)} %collective-permute-done.15.refs_10_), channel_id=1, source_target_pairs={{0,4},{4,0},{8,12},{12,8},{16,20},{20,16},{24,28},{28,24},{32,36},... | collective-permute-start | bytes 1179656 | tf_op jit(solution)/shard_map/ppermute | solution.py:39
  47.7 31.2 %all-to-all-start = ((bf16[4,64,960]{2,1,0:T(8,128)(2,1)}), bf16[4,64,960]{2,1,0:T(8,128)(2,1)S(1)}, u32[]{:S(2)}, u32[]{:S(2)}) async-start(bf16[4,64,960]{2,1,0:T(8,128)(2,1)} %bitcast.3), calls=%async_computation | async-start | bytes 1048576 | tf_op jit(solution)/shard_map/all_to_all | solution.py:44
  78.9 25.5 %all-to-all-start.1 = ((bf16[4,272,512]{2,1,0:T(8,128)(2,1)}), bf16[4,272,512]{2,1,0:T(8,128)(2,1)S(1)}, u32[]{:S(2)}, u32[]{:S(2)}) async-start(bf16[4,272,512]{2,1,0:T(8,128)(2,1)} %shard_map.138), calls=%async_computation.1 | async-start | bytes 2228224 | tf_op jit(solution)/shard_map/all_to_all | solution.py:51
  83.2 17.3 %collective-permute-start.1 = (bf16[3,64,960]{2,1,0:T(8,128)(2,1)S(1)}, bf16[3,64,960]{2,1,0:T(8,128)(2,1)S(1)}, u32[]{:S(2)}, u32[]{:S(2)}) collective-permute-start(bf16[3,64,960]{2,1,0:T(8,128)(2,1)S(1)} %pad_maximum_fusion.refs_0_), channel_id=1, source_target_pairs={{0,64},{4,68},{8,72},{12,76},{16,80},{20,84},{24,88},{28,92},{32,9... | collective-permute-start | bytes 1105928 | tf_op jit(solution)/shard_map/ppermute | solution.py:39
  83.3 20.6 %collective-permute-start.2 = (bf16[3,64,960]{2,1,0:T(8,128)(2,1)S(1)}, bf16[3,64,960]{2,1,0:T(8,128)(2,1)S(1)}, u32[]{:S(2)}, u32[]{:S(2)}) collective-permute-start(bf16[3,64,960]{2,1,0:T(8,128)(2,1)S(1)} %pad_maximum_fusion.refs_0_), channel_id=1, source_target_pairs={{0,192},{4,196},{8,200},{12,204},{16,208},{20,212},{24,216},{28,22... | collective-permute-start | bytes 1105928 | tf_op jit(solution)/shard_map/ppermute | solution.py:39
  85.3 18.6 %collective-permute-start.3 = (bf16[3,64,960]{2,1,0:T(8,128)(2,1)S(1)}, bf16[3,64,960]{2,1,0:T(8,128)(2,1)S(1)}, u32[]{:S(2)}, u32[]{:S(2)}) collective-permute-start(bf16[3,64,960]{2,1,0:T(8,128)(2,1)S(1)} %pad_maximum_fusion.refs_0_), channel_id=1, source_target_pairs={{0,128},{4,132},{8,136},{12,140},{16,144},{20,148},{24,152},{28,15... | collective-permute-start | bytes 1105928 | tf_op jit(solution)/shard_map/ppermute | solution.py:39
  85.3 23.2 %collective-permute-start.4 = (bf16[3,64,960]{2,1,0:T(8,128)(2,1)S(1)}, bf16[3,64,960]{2,1,0:T(8,128)(2,1)S(1)}, u32[]{:S(2)}, u32[]{:S(2)}) collective-permute-start(bf16[3,64,960]{2,1,0:T(8,128)(2,1)S(1)} %pad_maximum_fusion.refs_0_), channel_id=1, source_target_pairs={{0,4},{4,0},{8,12},{12,8},{16,20},{20,16},{24,28},{28,24},{32,36},... | collective-permute-start | bytes 1105928 | tf_op jit(solution)/shard_map/ppermute | solution.py:39
  100.5 9.6 %collective-permute-start.5 = (bf16[3,64,960]{2,1,0:T(8,128)(2,1)S(1)}, bf16[3,64,960]{2,1,0:T(8,128)(2,1)S(1)}, u32[]{:S(2)}, u32[]{:S(2)}) collective-permute-start(bf16[3,64,960]{2,1,0:T(8,128)(2,1)S(1)} %collective-permute-done.1.refs_1_), channel_id=1, source_target_pairs={{0,4},{4,0},{8,12},{12,8},{16,20},{20,16},{24,28},{28,24},{32,36},... | collective-permute-start | bytes 1105928 | tf_op jit(solution)/shard_map/ppermute | solution.py:39
  103.9 8.3 %collective-permute-start.6 = (bf16[3,64,960]{2,1,0:T(8,128)(2,1)S(1)}, bf16[3,64,960]{2,1,0:T(8,128)(2,1)}, u32[]{:S(2)}, u32[]{:S(2)}) collective-permute-start(bf16[3,64,960]{2,1,0:T(8,128)(2,1)S(1)} %collective-permute-done.2.refs_2_), channel_id=1, source_target_pairs={{0,4},{4,0},{8,12},{12,8},{16,20},{20,16},{24,28},{28,24},{32,36},... | collective-permute-start | bytes 1105928 | tf_op jit(solution)/shard_map/ppermute | solution.py:39
  103.9 22.9 %collective-permute-start.7 = (bf16[3,64,960]{2,1,0:T(8,128)(2,1)S(1)}, bf16[3,64,960]{2,1,0:T(8,128)(2,1)}, u32[]{:S(2)}, u32[]{:S(2)}) collective-permute-start(bf16[3,64,960]{2,1,0:T(8,128)(2,1)S(1)} %collective-permute-done.3.refs_3_), channel_id=1, source_target_pairs={{0,4},{4,0},{8,12},{12,8},{16,20},{20,16},{24,28},{28,24},{32,36},... | collective-permute-start | bytes 1105928 | tf_op jit(solution)/shard_map/ppermute | solution.py:39
  105.8 14.9 %collective-permute-start.25 = (bf16[128,512]{1,0:T(8,128)(2,1)}, bf16[128,512]{1,0:T(8,128)(2,1)S(1)}, u32[]{:S(2)}, u32[]{:S(2)}) collective-permute-start(bf16[128,512]{1,0:T(8,128)(2,1)} %get-tuple-element.24.refs_3_), channel_id=1, source_target_pairs={{0,1},{1,2},{2,3},{3,0},{4,5},{5,6},{6,7},{7,4},{8,9},{9,10},{10,1... | collective-permute-start | bytes 393224 | tf_op jit(solution)/shard_map/ppermute | solution.py:55
  108.5 12.8 %collective-permute-start.27 = (bf16[128,512]{1,0:T(8,128)(2,1)}, bf16[128,512]{1,0:T(8,128)(2,1)S(1)}, u32[]{:S(2)}, u32[]{:S(2)}) collective-permute-start(bf16[128,512]{1,0:T(8,128)(2,1)} %get-tuple-element.25.refs_4_), channel_id=1, source_target_pairs={{0,3},{1,0},{2,1},{3,2},{4,7},{5,4},{6,5},{7,6},{8,11},{9,8},{10,9... | collective-permute-start | bytes 393224 | tf_op jit(solution)/shard_map/ppermute | solution.py:55
  110.1 21.7 %collective-permute-start.29 = (bf16[128,512]{1,0:T(8,128)(2,1)}, bf16[128,512]{1,0:T(8,128)(2,1)S(1)}, u32[]{:S(2)}, u32[]{:S(2)}) collective-permute-start(bf16[128,512]{1,0:T(8,128)(2,1)} %get-tuple-element.25.refs_4_), channel_id=1, source_target_pairs={{0,1},{1,2},{2,3},{3,0},{4,5},{5,6},{6,7},{7,4},{8,9},{9,10},{10,1... | collective-permute-start | bytes 393224 | tf_op jit(solution)/shard_map/ppermute | solution.py:55
  112.2 19.6 %collective-permute-start.30 = (bf16[128,512]{1,0:T(8,128)(2,1)}, bf16[128,512]{1,0:T(8,128)(2,1)S(1)}, u32[]{:S(2)}, u32[]{:S(2)}) collective-permute-start(bf16[128,512]{1,0:T(8,128)(2,1)} %get-tuple-element.24.refs_3_), channel_id=1, source_target_pairs={{0,3},{1,0},{2,1},{3,2},{4,7},{5,4},{6,5},{7,6},{8,11},{9,8},{10,9... | collective-permute-start | bytes 393224 | tf_op jit(solution)/shard_map/ppermute | solution.py:55
  120.7 13.1 %collective-permute-start.26 = (bf16[128,512]{1,0:T(8,128)(2,1)S(1)}, bf16[128,512]{1,0:T(8,128)(2,1)S(1)}, u32[]{:S(2)}, u32[]{:S(2)}) collective-permute-start(bf16[128,512]{1,0:T(8,128)(2,1)S(1)} %collective-permute-done.25.refs_5_), channel_id=1, source_target_pairs={{0,1},{1,2},{2,3},{3,0},{4,5},{5,6},{6,7},{7,4},{8,9},{9,10},{10,1... | collective-permute-start | bytes 393224 | tf_op jit(solution)/shard_map/ppermute | solution.py:55
  121.3 12.5 %collective-permute-start.28 = (bf16[128,512]{1,0:T(8,128)(2,1)S(1)}, bf16[128,512]{1,0:T(8,128)(2,1)S(1)}, u32[]{:S(2)}, u32[]{:S(2)}) collective-permute-start(bf16[128,512]{1,0:T(8,128)(2,1)S(1)} %collective-permute-done.27.refs_8_), channel_id=1, source_target_pairs={{0,3},{1,0},{2,1},{3,2},{4,7},{5,4},{6,5},{7,6},{8,11},{9,8},{10,9... | collective-permute-start | bytes 393224 | tf_op jit(solution)/shard_map/ppermute | solution.py:55
  (12 other events, 218.2 us)
